TPU v7x, 512 devices: a whole 4x8x8 slice. The times are simulated.
512 devices in a mesh: clip: 64 (over z, y_hi, x), val: 8 (over y_lo, core).
Axes of the slice: x: 4, y: 8 (y_hi: 2, y_lo: 4; y = y_hi * 4 + y_lo), z: 8, core: 2. Of those that a mesh axis runs over, the one named last changes fastest.
Arguments:
- latents: bfloat16 [1024, 8192], P('clip', 'val'), may hold values from -10 to 10
- noise: bfloat16 [1024, 8192], P('clip', 'val'), may hold values from -10 to 10
- offsets: int32 [1024, 2, 2], P('clip'), may hold values from 0 to 15
- times: float32 [1024], P('clip'), may hold values from 0.05 to 0.95
- embed: bfloat16 [64, 5120], replicated, may hold values from -0.75 to 0.75
Outputs:
- embedded: bfloat16 [1024, 128, 5120], P('clip', 'val')
All inputs are finite; a program needn't handle non-finite values.
Results may differ from a plain program's by a relative error of at most 0.0051.
Values may be sent and summed in bfloat16 or wider, within the bound.
A program may use at most 64 MiB of HBM per device.

v0:
```python
import math
import jax
import jax.numpy as jnp
from jax import lax
from jax.sharding import PartitionSpec as P

P_SIZE = 64
FR = 2
GW = 16
GH = 4
ITERS = 4
S = 128


def warp_noise(noise, offsets):
    clips = noise.shape[0]
    tokens = FR * GH * GW
    value_cube = noise.reshape(clips, noise.shape[1] // tokens, tokens)
    shift_y = offsets[:, :, 0] % GH
    shift_x = offsets[:, :, 1] % GW
    src_rows = (jnp.arange(GH, dtype=jnp.int32)[None, None, :] - shift_y[:, :, None]) % GH
    src_cols = (jnp.arange(GW, dtype=jnp.int32)[None, None, :] - shift_x[:, :, None]) % GW
    frame_base = (jnp.arange(FR, dtype=jnp.int32) * (GH * GW))[None, :, None, None]
    source = (frame_base + src_rows[:, :, :, None] * GW + src_cols[:, :, None, :]).reshape(
        clips, tokens
    )
    source = jnp.broadcast_to(source[:, None, :], value_cube.shape)
    return jnp.take_along_axis(value_cube, source, axis=2).reshape(noise.shape)


def row_stats(scores):
    top = jnp.max(scores, axis=1)
    total = jnp.sum(jnp.exp(scores - top[:, None]), axis=1)
    return (top, total)


def column_lse(scores):
    top = jnp.max(scores, axis=0)
    top = lax.pmax(top, "clip")
    total = lax.psum(jnp.sum(jnp.exp(scores - top[None, :]), axis=0), "clip")
    return top + jnp.log(total)


def on_device(latents, noise, offsets, times, embed):
    warped = warp_noise(noise, offsets)
    clips = latents.shape[0]
    volume = P_SIZE * S
    entropy = 0.5 / math.sqrt(volume)
    contract = (((1,), (1,)), ((), ()))
    panel_all = lax.all_gather(warped, "clip", axis=0, tiled=True)
    gram_part = lax.dot_general(latents, panel_all, contract, preferred_element_type=jnp.float32)
    square_part = jnp.sum(jnp.square(panel_all.astype(jnp.float32)), axis=1)
    gram, square = lax.psum((gram_part, square_part), "val")
    cost = (square[None, :] - 2.0 * gram) / volume
    column_dual = jnp.zeros((cost.shape[1],), jnp.float32)
    for sweep_index in range(ITERS):
        top, total = row_stats((column_dual[None, :] - cost) / entropy)
        row_dual = -entropy * (top + jnp.log(total))
        column_dual = -entropy * column_lse((row_dual[:, None] - cost) / entropy)
    scores = (column_dual[None, :] - cost) / entropy
    top, total = row_stats(scores)
    weights = (jnp.exp(scores - top[:, None]) / total[:, None]).astype(jnp.bfloat16)
    coupled = jnp.dot(weights, panel_all, preferred_element_type=jnp.float32)
    mixed = (
        (1.0 - times)[:, None] * latents.astype(jnp.float32) + times[:, None] * coupled
    ).astype(jnp.bfloat16)
    value_cube = mixed.reshape(clips, latents.shape[1] // S, S)
    return jnp.einsum(
        "cps,pd->csd",
        lax.all_to_all(value_cube, "val", split_axis=2, concat_axis=1, tiled=True),
        embed,
        preferred_element_type=jnp.float32,
    ).astype(jnp.bfloat16)


def solution(mesh):
    placed = (P("clip", "val"), P("clip", "val"), P("clip", None, None), P("clip"), P())
    return jax.shard_map(
        on_device, mesh=mesh, in_specs=placed, out_specs=P("clip", "val", None), check_vma=False
    )
```

profile of v0, /device:TPU:1, one launch (start us, length us, event | category | flops | bytes accessed | tf_op | source)
XLA Modules:
  0.0 2139.3 jit_solution(8296339982809576350)
XLA Ops:
  6.5 0.8 and_select_fusion.3
  7.3 0.1 copy.29
  7.4 0.1 copy.28
  7.5 0.1 and_select_fusion
  7.6 0.1 fusion.22
  7.7 0.1 broadcast_add_fusion
  7.8 0.1 add.138
  7.9 0.8 copy.37
  8.7 145.1 %gather_fusion = bf16[16384]{0:T(1024)(128)(2,1)S(1)} fusion(bf16[16,8,128]{2,1,0:T(8,128)(2,1)S(1)} %bitcast.32, s32[16384]{0:T(1024)S(1)} %or_bitcast_fusion), kind=kCustom, calls=%fused_computation | custom fusion | bytes 262144 | tf_op jit(solution)/shard_map/jit(take_along_axis)/gather | solution.py:28
  153.9 0.6 copy.41
  154.6 135.1 %all-gather.2.cloned.1.call-done = bf16[1024,1024]{1,0:T(8,128)(2,1)} async-done(((bf16[16,1024]{1,0:T(8,128)(2,1)}), bf16[1024,1024]{1,0:T(8,128)(2,1)}) %all-gather.2.cloned.1.call-update) | async-done | bytes 2097168 | tf_op jit(solution)/shard_map/all_gather | solution.py:50
  289.7 3.0 convolution_bitcast_fusion
  292.8 0.5 multiply_reduce_fusion
  293.3 17.5 psum.42
  310.8 55.7 %all-reduce.2.cloned.1.call-done = f32[16,1024]{1,0:T(8,128)} async-done(((f32[16,1024]{1,0:T(8,128)}), f32[16,1024]{1,0:T(8,128)}) %all-reduce.2.cloned.1.call-update) | async-done | bytes 65552 | tf_op jit(solution)/shard_map/psum | solution.py:53
  366.5 1.0 fusion.7
  367.5 1.0 exponential_reduce_fusion.7
  368.5 0.9 fusion.8
  369.4 197.3 %pmax.28 = f32[1024]{0:T(1024)S(1)} all-reduce(f32[1024]{0:T(1024)S(1)} %fusion.8), channel_id=1, replica_groups=mesh['clip'=64,'val'=8] {'clip'}, use_global_device_ids=true, to_apply=%region_6.7 | all-reduce | flops 1024 | bytes 8192 | tf_op jit(solution)/shard_map/pmax | solution.py:39
  566.7 0.9 exponential_reduce_fusion.6
  567.6 187.5 %psum.44 = f32[1024]{0:T(1024)S(1)} all-reduce(f32[1024]{0:T(1024)S(1)} %exponential_reduce_fusion.6), channel_id=1, replica_groups=mesh['clip'=64,'val'=8] {'clip'}, use_global_device_ids=true, to_apply=%region_8.9 | all-reduce | flops 1024 | bytes 8192 | tf_op jit(solution)/shard_map/psum | solution.py:40
  755.2 1.0 fusion.9
  756.1 1.0 exponential_reduce_fusion.5
  757.2 0.9 fusion.10
  758.1 188.7 %pmax.29 = f32[1024]{0:T(1024)S(1)} all-reduce(f32[1024]{0:T(1024)S(1)} %fusion.10), channel_id=1, replica_groups=mesh['clip'=64,'val'=8] {'clip'}, use_global_device_ids=true, to_apply=%region_12.13 | all-reduce | flops 1024 | bytes 8192 | tf_op jit(solution)/shard_map/pmax | solution.py:39
  946.8 0.9 exponential_reduce_fusion.4
  947.8 187.4 %psum.45 = f32[1024]{0:T(1024)S(1)} all-reduce(f32[1024]{0:T(1024)S(1)} %exponential_reduce_fusion.4), channel_id=1, replica_groups=mesh['clip'=64,'val'=8] {'clip'}, use_global_device_ids=true, to_apply=%region_14.15 | all-reduce | flops 1024 | bytes 8192 | tf_op jit(solution)/shard_map/psum | solution.py:40
  1135.1 1.0 fusion.11
  1136.1 1.0 exponential_reduce_fusion.3
  1137.2 0.9 fusion.12
  1138.1 189.1 %pmax.30 = f32[1024]{0:T(1024)S(1)} all-reduce(f32[1024]{0:T(1024)S(1)} %fusion.12), channel_id=1, replica_groups=mesh['clip'=64,'val'=8] {'clip'}, use_global_device_ids=true, to_apply=%region_18.19 | all-reduce | flops 1024 | bytes 8192 | tf_op jit(solution)/shard_map/pmax | solution.py:39
  1327.2 0.9 exponential_reduce_fusion.2
  1328.2 187.5 %psum.46 = f32[1024]{0:T(1024)S(1)} all-reduce(f32[1024]{0:T(1024)S(1)} %exponential_reduce_fusion.2), channel_id=1, replica_groups=mesh['clip'=64,'val'=8] {'clip'}, use_global_device_ids=true, to_apply=%region_20.21 | all-reduce | flops 1024 | bytes 8192 | tf_op jit(solution)/shard_map/psum | solution.py:40
  1515.7 1.0 fusion.13
  1516.7 1.0 exponential_reduce_fusion.1
  1517.7 0.9 fusion.14
  1518.7 189.0 %pmax.31 = f32[1024]{0:T(1024)S(1)} all-reduce(f32[1024]{0:T(1024)S(1)} %fusion.14), channel_id=1, replica_groups=mesh['clip'=64,'val'=8] {'clip'}, use_global_device_ids=true, to_apply=%region_24.25 | all-reduce | flops 1024 | bytes 8192 | tf_op jit(solution)/shard_map/pmax | solution.py:39
  1707.7 0.9 exponential_reduce_fusion
  1708.6 187.5 %psum.47 = f32[1024]{0:T(1024)S(1)} all-reduce(f32[1024]{0:T(1024)S(1)} %exponential_reduce_fusion), channel_id=1, replica_groups=mesh['clip'=64,'val'=8] {'clip'}, use_global_device_ids=true, to_apply=%region_26.27 | all-reduce | flops 1024 | bytes 8192 | tf_op jit(solution)/shard_map/psum | solution.py:40
  1896.1 1.0 fusion.15
  1897.1 1.0 fusion.16
  1898.1 1.3 fusion.2
  1899.4 0.2 copy.30
  1899.6 0.3 reshape.134
  1899.9 229.7 %all_to_all.18 = bf16[8,2,1024]{2,1,0:T(2,128)(2,1)S(1)} all-to-all(bf16[8,2,1024]{2,1,0:T(2,128)(2,1)S(1)} %reshape.134), channel_id=1, replica_groups=mesh['clip'=64,'val'=8] {'val'}, dimensions={0} | all-to-all | bytes 65536 | tf_op jit(solution)/shard_map/all_to_all | solution.py:70
  2129.5 0.2 reshape.135
  2129.8 0.6 copy.32
  2130.3 2.1 convolution_convert_fusion
  (27 shorter events, 0.3 us)
Async XLA Ops:
  6.5 2123.8 %copy-start = (bf16[64,5120]{1,0:T(8,128)(2,1)S(1)}, bf16[64,5120]{1,0:T(8,128)(2,1)}, u32[]{:S(2)}) copy-start(bf16[64,5120]{1,0:T(8,128)(2,1)} %param.9) | copy-start | bytes 1966084
  6.5 283.2 %all-gather.2.cloned.1.call-start = ((), (), s32[]{:S(2)}) async-start(), calls=%async_computation.1 | async-start | bytes 2129920 | tf_op jit(solution)/shard_map/all_gather | solution.py:50
  8.7 145.9 %copy-start.3 = (f32[16]{0:T(128)S(1)}, f32[16]{0:T(128)}, u32[]{:S(2)}) copy-start(f32[16]{0:T(128)} %param.8) | copy-start | bytes 196
  8.7 281.0 %copy-start.2 = (bf16[16,1024]{1,0:T(8,128)(2,1)S(1)}, bf16[16,1024]{1,0:T(8,128)(2,1)}, u32[]{:S(2)}) copy-start(bf16[16,1024]{1,0:T(8,128)(2,1)} %param.5) | copy-start | bytes 98308
  154.5 212.0 %all-reduce.2.cloned.1.call-start = ((), (), s32[]{:S(2)}) async-start(), calls=%async_computation.2 | async-start | bytes 131072 | tf_op jit(solution)/shard_map/psum | solution.py:53
  289.7 3.1 copy-start.1
Sparse Core Ops, SparseCore 0:
  154.7 135.0 all-gather.1
  292.9 73.5 all-reduce.1
where the time goes:
time: 2140 us
  blocking collectives  1760 us (82%)
  waiting for transfers between devices  191 us (9%)
  local copies, waits for them, and re-layouts  148 us (7%)
    pmax x4, blocking collectives, column_lse(): top = lax.pmax(top, 'clip')  764 us
    psum x4, blocking collectives, column_lse(): total = lax.psum(jnp.sum(jnp.exp(scores - top[None, :]), axis=0), 'clip')  750 us
    all_to_all x1, blocking collectives, on_device(): lax.all_to_all(value_cube, 'val', split_axis=2, concat_axis=1, tiled=True)  230 us
    gather x1, local copies, waits for them, and re-layouts, warp_noise(): return jnp.take_along_axis(value_cube, source, axis=2).reshape(noise.shape)  145 us
    all_gather x1, waiting for transfers between devices, on_device(): panel_all = lax.all_gather(warped, 'clip', axis=0, tiled=True)  135 us
    psum x1, waiting for transfers between devices, on_device(): gram, square = lax.psum((gram_part, square_part), 'val')  55.7 us
  transfers between devices with their start and end apart: 2, of which 2 were waited for; matrix products, arithmetic and copies ran while one was open for 0% of the time, Pallas kernels for 0%

commit v1 on v0

--- a/solution.py
+++ b/solution.py
@@ -47,7 +47,10 @@
     volume = P_SIZE * S
     entropy = 0.5 / math.sqrt(volume)
     contract = (((1,), (1,)), ((), ()))
-    panel_all = lax.all_gather(warped, "clip", axis=0, tiled=True)
+    devices = lax.axis_size("clip")
+    tiles = jnp.stack([warped for _ in range(devices)])
+    tiles = lax.all_to_all(tiles, "clip", split_axis=0, concat_axis=0)
+    panel_all = jnp.concatenate(tiles, axis=0)
     gram_part = lax.dot_general(latents, panel_all, contract, preferred_element_type=jnp.float32)
     square_part = jnp.sum(jnp.square(panel_all.astype(jnp.float32)), axis=1)
     gram, square = lax.psum((gram_part, square_part), "val")

time: 2140 us -> 2080 us (0.972)
  waiting for transfers between devices: 191 us -> 104 us
    all_gather x1 -> x0, waiting for transfers between devices: 135 us -> none  [on_device(): panel_all = lax.all_gather(warped, 'clip', axis=0, tiled=True)]
    all_to_all x0 -> x1, waiting for transfers between devices: none -> 49.2 us  [on_device(): tiles = lax.all_to_all(tiles, 'clip', split_axis=0, concat_axis=0)]
where the time goes in v1:
time: 2080 us; the launch traced here: 2070 us
  blocking collectives  1760 us (85%)
  local copies, waits for them, and re-layouts  149 us (7%)
  waiting for transfers between devices  104 us (5%)
    pmax x4, blocking collectives, column_lse(): top = lax.pmax(top, 'clip')  764 us
    psum x4, blocking collectives, column_lse(): total = lax.psum(jnp.sum(jnp.exp(scores - top[None, :]), axis=0), 'clip')  750 us
    all_to_all x1, blocking collectives, on_device(): lax.all_to_all(value_cube, 'val', split_axis=2, concat_axis=1, tiled=True)  230 us
    gather x1, local copies, waits for them, and re-layouts, warp_noise(): return jnp.take_along_axis(value_cube, source, axis=2).reshape(noise.shape)  145 us
    psum x1, waiting for transfers between devices, on_device(): gram, square = lax.psum((gram_part, square_part), 'val')  54.7 us
    all_to_all x1, waiting for transfers between devices, on_device(): tiles = lax.all_to_all(tiles, 'clip', split_axis=0, concat_axis=0)  49.2 us
  transfers between devices with their start and end apart: 2, of which 2 were waited for; matrix products, arithmetic and copies ran while one was open for 0% of the time, Pallas kernels for 0%

profile of v1, /device:TPU:1, one launch (start us, length us, event | category | flops | bytes accessed | tf_op | source)
XLA Modules:
  0.0 2073.6 jit_solution(15573309284947173162)
XLA Ops:
  6.5 0.8 and_select_fusion.3
  7.3 0.1 copy.28
  7.5 0.1 and_select_fusion
  7.6 0.1 fusion.22
  7.7 0.1 broadcast_add_fusion
  7.8 0.1 add.138
  7.9 0.8 copy.37
  8.7 145.1 %gather_fusion = bf16[16384]{0:T(1024)(128)(2,1)S(1)} fusion(bf16[16,8,128]{2,1,0:T(8,128)(2,1)S(1)} %bitcast.33, s32[16384]{0:T(1024)S(1)} %or_bitcast_fusion), kind=kCustom, calls=%fused_computation | custom fusion | bytes 262144 | tf_op jit(solution)/shard_map/jit(take_along_axis)/gather | solution.py:28
  153.9 1.6 stack.3
  155.5 19.7 all-to-all-start
  175.3 49.2 %all-to-all-done = bf16[64,16,1024]{2,1,0:T(8,128)(2,1)S(1)} async-done(((bf16[64,16,1024]{2,1,0:T(8,128)(2,1)}), bf16[64,16,1024]{2,1,0:T(8,128)(2,1)S(1)}, u32[]{:S(2)}, u32[]{:S(2)}) %all-to-all-start) | async-done | bytes 2097184 | tf_op jit(solution)/shard_map/all_to_all | solution.py:52
  224.5 1.3 convolution_bitcast_fusion
  225.8 0.5 multiply_reduce_fusion
  226.3 19.7 psum.42
  246.1 54.7 %all-reduce.2.cloned.1.call-done = f32[16,1024]{1,0:T(8,128)} async-done(((f32[16,1024]{1,0:T(8,128)}), f32[16,1024]{1,0:T(8,128)}) %all-reduce.2.cloned.1.call-update) | async-done | bytes 65552 | tf_op jit(solution)/shard_map/psum | solution.py:56
  300.8 1.0 fusion.7
  301.8 1.0 exponential_reduce_fusion.7
  302.8 0.9 fusion.8
  303.7 197.3 %pmax.28 = f32[1024]{0:T(1024)S(1)} all-reduce(f32[1024]{0:T(1024)S(1)} %fusion.8), channel_id=1, replica_groups=mesh['clip'=64,'val'=8] {'clip'}, use_global_device_ids=true, to_apply=%region_6.7 | all-reduce | flops 1024 | bytes 8192 | tf_op jit(solution)/shard_map/pmax | solution.py:39
  501.0 0.9 exponential_reduce_fusion.6
  501.9 187.5 %psum.44 = f32[1024]{0:T(1024)S(1)} all-reduce(f32[1024]{0:T(1024)S(1)} %exponential_reduce_fusion.6), channel_id=1, replica_groups=mesh['clip'=64,'val'=8] {'clip'}, use_global_device_ids=true, to_apply=%region_8.9 | all-reduce | flops 1024 | bytes 8192 | tf_op jit(solution)/shard_map/psum | solution.py:40
  689.5 1.0 fusion.9
  690.4 1.0 exponential_reduce_fusion.5
  691.5 0.9 fusion.10
  692.4 188.7 %pmax.29 = f32[1024]{0:T(1024)S(1)} all-reduce(f32[1024]{0:T(1024)S(1)} %fusion.10), channel_id=1, replica_groups=mesh['clip'=64,'val'=8] {'clip'}, use_global_device_ids=true, to_apply=%region_12.13 | all-reduce | flops 1024 | bytes 8192 | tf_op jit(solution)/shard_map/pmax | solution.py:39
  881.1 0.9 exponential_reduce_fusion.4
  882.0 187.4 %psum.45 = f32[1024]{0:T(1024)S(1)} all-reduce(f32[1024]{0:T(1024)S(1)} %exponential_reduce_fusion.4), channel_id=1, replica_groups=mesh['clip'=64,'val'=8] {'clip'}, use_global_device_ids=true, to_apply=%region_14.15 | all-reduce | flops 1024 | bytes 8192 | tf_op jit(solution)/shard_map/psum | solution.py:40
  1069.4 1.0 fusion.11
  1070.4 1.0 exponential_reduce_fusion.3
  1071.5 0.9 fusion.12
  1072.4 189.1 %pmax.30 = f32[1024]{0:T(1024)S(1)} all-reduce(f32[1024]{0:T(1024)S(1)} %fusion.12), channel_id=1, replica_groups=mesh['clip'=64,'val'=8] {'clip'}, use_global_device_ids=true, to_apply=%region_18.19 | all-reduce | flops 1024 | bytes 8192 | tf_op jit(solution)/shard_map/pmax | solution.py:39
  1261.5 0.9 exponential_reduce_fusion.2
  1262.5 187.5 %psum.46 = f32[1024]{0:T(1024)S(1)} all-reduce(f32[1024]{0:T(1024)S(1)} %exponential_reduce_fusion.2), channel_id=1, replica_groups=mesh['clip'=64,'val'=8] {'clip'}, use_global_device_ids=true, to_apply=%region_20.21 | all-reduce | flops 1024 | bytes 8192 | tf_op jit(solution)/shard_map/psum | solution.py:40
  1450.0 1.0 fusion.13
  1451.0 1.0 exponential_reduce_fusion.1
  1452.0 0.9 fusion.14
  1453.0 189.0 %pmax.31 = f32[1024]{0:T(1024)S(1)} all-reduce(f32[1024]{0:T(1024)S(1)} %fusion.14), channel_id=1, replica_groups=mesh['clip'=64,'val'=8] {'clip'}, use_global_device_ids=true, to_apply=%region_24.25 | all-reduce | flops 1024 | bytes 8192 | tf_op jit(solution)/shard_map/pmax | solution.py:39
  1642.0 0.9 exponential_reduce_fusion
  1642.9 187.5 %psum.47 = f32[1024]{0:T(1024)S(1)} all-reduce(f32[1024]{0:T(1024)S(1)} %exponential_reduce_fusion), channel_id=1, replica_groups=mesh['clip'=64,'val'=8] {'clip'}, use_global_device_ids=true, to_apply=%region_26.27 | all-reduce | flops 1024 | bytes 8192 | tf_op jit(solution)/shard_map/psum | solution.py:40
  1830.4 1.0 fusion.15
  1831.3 1.0 fusion.16
  1832.4 1.3 fusion.2
  1833.7 0.2 copy.30
  1833.9 0.3 reshape.143
  1834.2 229.7 %all_to_all.23 = bf16[8,2,1024]{2,1,0:T(2,128)(2,1)S(1)} all-to-all(bf16[8,2,1024]{2,1,0:T(2,128)(2,1)S(1)} %reshape.143), channel_id=1, replica_groups=mesh['clip'=64,'val'=8] {'val'}, dimensions={0} | all-to-all | bytes 65536 | tf_op jit(solution)/shard_map/all_to_all | solution.py:73
  2063.8 0.2 reshape.144
  2064.1 0.6 copy.32
  2064.6 2.1 convolution_convert_fusion
  (26 shorter events, 0.4 us)
Async XLA Ops:
  6.5 2058.1 %copy-start = (bf16[64,5120]{1,0:T(8,128)(2,1)S(1)}, bf16[64,5120]{1,0:T(8,128)(2,1)}, u32[]{:S(2)}) copy-start(bf16[64,5120]{1,0:T(8,128)(2,1)} %param.9) | copy-start | bytes 1966084
  155.5 19.8 copy-start.2
  155.5 69.0 %copy-start.1 = (bf16[16,1024]{1,0:T(8,128)(2,1)S(1)}, bf16[16,1024]{1,0:T(8,128)(2,1)}, u32[]{:S(2)}) copy-start(bf16[16,1024]{1,0:T(8,128)(2,1)} %param.5) | copy-start | bytes 98308
  155.5 69.0 %all-to-all-start = ((bf16[64,16,1024]{2,1,0:T(8,128)(2,1)}), bf16[64,16,1024]{2,1,0:T(8,128)(2,1)S(1)}, u32[]{:S(2)}, u32[]{:S(2)}) async-start(bf16[64,16,1024]{2,1,0:T(8,128)(2,1)} %stack.3), calls=%async_computation | async-start | bytes 4194304 | tf_op jit(solution)/shard_map/all_to_all | solution.py:52
  175.2 125.6 %all-reduce.2.cloned.1.call-start = ((), (), s32[]{:S(2)}) async-start(), calls=%async_computation.2 | async-start | bytes 131072 | tf_op jit(solution)/shard_map/psum | solution.py:56
Sparse Core Ops, SparseCore 0:
  225.9 74.8 all-reduce.1
